TPU v7x, 256 devices: a whole 4x4x8 slice. The times are simulated.
256 devices in a mesh: batch: 8 (over z), col: 32 (over y, x, core).
Axes of the slice: x: 4, y: 4, z: 8, core: 2. Of those that a mesh axis runs over, the one named last changes fastest.
Arguments:
- views: bfloat16 [2, 1024, 4096], P(None, 'batch', 'col'), may hold values from -132 to 132
- norm_scale_gain: float32 [4096], P('col'), may hold values from 0.5 to 1.5
- norm_shift_bias: float32 [4096], P('col'), may hold values from -3 to 3
- weight: bfloat16 [4096, 8192], P(None, 'col'), may hold values from -0.09375 to 0.09375
Outputs:
- loss: float32 [], replicated
- grad_weight: float32 [4096, 8192], P('batch', 'col')
- grad_gain: float32 [4096], P('col')
- grad_bias: float32 [4096], P('col')
- views_gradient: float32 [2, 1024, 4096], P(None, 'batch', 'col')
All inputs are finite; a program needn't handle non-finite values.
Results may differ from a plain program's by a relative error of at most 0.0027.
Values may be sent and summed in bfloat16 or wider, within the bound.
A program may use at most 64 MiB of HBM per device.

v0:
```python
import jax
import jax.numpy as jnp
from jax import lax
from jax.sharding import PartitionSpec as P

E = 8192
eps_norm = 1e-05
eps_std = 0.0001


def gelu_slope(preactivation):
    value, pullback = jax.vjp(lambda t: jax.nn.gelu(t, approximate=True), preactivation)
    return pullback(jnp.ones_like(value))[0]


def shards(views, norm_scale_gain, norm_shift_bias, weight):
    n_batch = lax.axis_size("batch")
    n_col = lax.axis_size("col")
    local_rows = views.shape[1]
    sample_count = local_rows * n_batch
    scale = sample_count * E / 128.0
    hidden_float = views.astype(jnp.float32)
    total = lax.psum(jnp.sum(hidden_float, axis=1), "batch")
    batch_average = total[:, None, :] / sample_count
    centred = hidden_float - batch_average
    spread = lax.psum(jnp.sum(centred * centred, axis=1), "batch")
    var = spread[:, None, :] / sample_count
    inverse_deviation = 1.0 / jnp.sqrt(var + eps_norm)
    normalised_input = (hidden_float - batch_average) * inverse_deviation
    preactivation = norm_scale_gain * normalised_input + norm_shift_bias
    act = jax.nn.gelu(preactivation, approximate=True).astype(jnp.bfloat16)
    act_full = lax.all_gather(act, "col", axis=2, tiled=True)
    z_local = jnp.einsum(
        "vrk,kj->vrj", act_full, weight, preferred_element_type=jnp.float32
    ).astype(jnp.bfloat16)
    z_all = lax.all_gather(z_local, "batch", axis=1, tiled=True)
    zf_all = z_all.astype(jnp.float32)
    zmean = jnp.mean(zf_all, axis=1, keepdims=True)
    zc_all = zf_all - zmean
    zvar = jnp.sum(zc_all * zc_all, axis=1, keepdims=True) / (sample_count - 1)
    std = jnp.sqrt(zvar + eps_std)
    zcb_all = zc_all.astype(jnp.bfloat16)
    offset = lax.axis_index("batch") * local_rows
    zc_loc = lax.dynamic_slice_in_dim(zc_all, offset, local_rows, 1)
    zcb_loc = zc_loc.astype(jnp.bfloat16)
    diag = jnp.sum(jnp.square(zcb_all.astype(jnp.float32)), axis=1, keepdims=True)
    kernel_part = jnp.einsum("vrj,vmj->vrm", zcb_loc, zcb_all, preferred_element_type=jnp.float32)
    kernel = lax.psum(kernel_part, "col")
    kernel_b = kernel.astype(jnp.bfloat16)
    denom = float((sample_count - 1) ** 2 * E)
    coef = 4.0 * scale / denom
    hinge_coef = 25.0 * scale / (2.0 * E * (sample_count - 1))
    mask = jnp.where(std < 1.0, 1.0, 0.0)
    moved = jnp.einsum("vrm,vmj->vrj", kernel_b, zcb_all, preferred_element_type=jnp.float32)
    g_cov = coef * (moved - zcb_loc.astype(jnp.float32) * diag)
    g_var = -hinge_coef * mask * zc_loc / std
    summed = g_cov + g_var
    col_total = lax.psum(jnp.sum(summed, axis=1), "batch")
    zf_loc = z_local.astype(jnp.float32)
    diff = zf_loc[0] - zf_loc[1]
    g_inv = 50.0 * scale / (sample_count * E) * diff
    dz = summed - col_total[:, None, :] / sample_count + jnp.stack([g_inv, -g_inv])
    dzb = dz.astype(jnp.bfloat16)
    inv_share = jnp.sum(diff * diff) / (sample_count * E)
    hinge_share = jnp.sum(jnp.maximum(1.0 - std, 0.0)) / (2 * E)
    block_share = jnp.sum(kernel * kernel) / denom
    diag_share = jnp.sum(diag * diag) / denom
    share = 25.0 * inv_share + (25.0 * hinge_share - diag_share) / n_batch + block_share / n_col
    loss = lax.psum(share, ("batch", "col"))
    d_act_t = lax.psum_scatter(
        jnp.einsum("kj,vrj->kvr", weight, dzb, preferred_element_type=jnp.float32),
        "col",
        scatter_dimension=0,
        tiled=True,
    )
    d_act = jnp.transpose(d_act_t, (1, 2, 0))
    grad_weight = lax.psum_scatter(
        jnp.einsum("vrk,vrj->kj", act_full, dzb, preferred_element_type=jnp.float32),
        "batch",
        scatter_dimension=0,
        tiled=True,
    )
    preactivation_gradient = d_act * gelu_slope(preactivation)
    bias_gradient_sum, gain_gradient_sum = lax.psum(
        (
            jnp.sum(preactivation_gradient, axis=1),
            jnp.sum(preactivation_gradient * normalised_input, axis=1),
        ),
        "batch",
    )
    grad_bias = jnp.sum(bias_gradient_sum, axis=0)
    grad_gain = jnp.sum(gain_gradient_sum, axis=0)
    views_gradient = (
        norm_scale_gain
        * (
            preactivation_gradient
            - bias_gradient_sum[:, None, :] / sample_count
            - normalised_input * gain_gradient_sum[:, None, :] / sample_count
        )
        * inverse_deviation
    )
    return (loss, grad_weight, grad_gain, grad_bias, views_gradient)


def solution(mesh):
    placed = (P(None, "batch", "col"), P("col"), P("col"), P(None, "col"))
    return jax.shard_map(
        shards,
        mesh=mesh,
        in_specs=placed,
        out_specs=(P(), P("batch", "col"), P("col"), P("col"), P(None, "batch", "col")),
        check_vma=False,
    )
```

profile of v0, /device:TPU:1, one launch (start us, length us, event | category | flops | bytes accessed | tf_op | source)
XLA Modules:
  0.0 430.3 jit_solution(8545685748164966906)
XLA Ops:
  7.2 0.0 copy-start
  7.2 0.0 all-gather.3.cloned.1.call-start
  7.2 1.0 convert_reduce_fusion.1
  8.2 17.3 %psum.49 = f32[2,128]{1,0:T(2,128)S(1)} all-reduce(f32[2,128]{1,0:T(2,128)S(1)} %convert_reduce_fusion.1), channel_id=1, replica_groups=mesh['batch'=8,'col'=32] {'batch'}, use_global_device_ids=true, to_apply=%region_1.0 | all-reduce | flops 256 | bytes 2048 | tf_op jit(solution)/shard_map/psum | solution.py:23
  25.5 0.9 fusion.32
  26.4 10.8 %psum.50 = f32[2,128]{1,0:T(2,128)S(1)} all-reduce(f32[2,128]{1,0:T(2,128)S(1)} %fusion.32), channel_id=1, replica_groups=mesh['batch'=8,'col'=32] {'batch'}, use_global_device_ids=true, to_apply=%region_3.0 | all-reduce | flops 256 | bytes 2048 | tf_op jit(solution)/shard_map/psum | solution.py:26
  37.2 1.6 fusion.25
  38.8 0.0 all-gather.3.cloned.1.call-update
  38.8 0.0 all-gather.5.cloned.1.call-start
  38.8 56.4 %all-gather.3.cloned.1.call-done = bf16[2,128,4096]{2,1,0:T(8,128)(2,1)} async-done(((bf16[2,128,128]{2,1,0:T(8,128)(2,1)}), bf16[2,128,4096]{2,1,0:T(8,128)(2,1)}) %all-gather.3.cloned.1.call-update) | async-done | bytes 2097168 | tf_op jit(solution)/shard_map/all_gather | solution.py:32
  95.2 0.0 copy-done
  95.2 3.0 fusion.42
  98.2 0.0 all-gather.5.cloned.1.call-update
  98.2 0.0 all-reduce.3.cloned.1.call-start
  98.2 32.8 %all-gather.5.cloned.1.call-done = bf16[2,1024,256]{2,1,0:T(8,128)(2,1)} async-done(((bf16[2,128,256]{2,1,0:T(8,128)(2,1)}), bf16[2,1024,256]{2,1,0:T(8,128)(2,1)}) %all-gather.5.cloned.1.call-update) | async-done | bytes 1048592 | tf_op jit(solution)/shard_map/all_gather | solution.py:36
  131.1 1.5 convert_reduce_fusion
  132.6 2.1 multiply_reduce_fusion
  134.7 1.3 copy-done.2
  136.0 0.0 copy-done.1
  136.0 1.5 fusion.10
  137.5 0.0 all-reduce.3.cloned.1.call-update
  137.5 0.0 reduce-scatter.5.cloned.1.call-start
  137.6 1.3 fusion.41
  138.8 1.3 fusion.37
  140.2 115.7 %all-reduce.3.cloned.1.call-done = f32[2,128,1024]{2,1,0:T(8,128)} async-done(((f32[2,128,1024]{2,1,0:T(8,128)}), f32[2,128,1024]{2,1,0:T(8,128)}) %all-reduce.3.cloned.1.call-update) | async-done | bytes 1048592 | tf_op jit(solution)/shard_map/psum | solution.py:48
  255.9 2.4 fusion.43
  258.3 13.7 %psum.53 = f32[2,256]{1,0:T(2,128)S(1)} all-reduce(f32[2,256]{1,0:T(2,128)S(1)} %get-tuple-element.23), channel_id=1, replica_groups=mesh['batch'=8,'col'=32] {'batch'}, use_global_device_ids=true, to_apply=%region_14.15 | all-reduce | flops 512 | bytes 4096 | tf_op jit(solution)/shard_map/psum | solution.py:58
  272.0 0.0 copy-done.5
  272.0 1.0 fusion.13
  272.9 2.7 convolution_bitcast_fusion
  275.7 0.0 reduce-scatter.5.cloned.1.call-update
  275.7 0.0 reduce-scatter.3.cloned.1.call-start
  275.7 4.3 convolution_bitcast_fusion.1
  280.0 0.0 reduce-scatter.3.cloned.1.call-update
  281.4 0.6 multiply_reduce_fusion.4
  282.7 0.0 copy-done.4
  282.7 0.9 multiply_reduce_fusion.2
  284.2 78.4 %psum.52 = f32[]{:T(128)} all-reduce(f32[]{:T(128)S(6)} %add.83), channel_id=1, replica_groups=mesh['batch'=8,'col'=32] {'batch','col'}, use_global_device_ids=true, to_apply=%region_12.13 | all-reduce | flops 1 | bytes 8 | tf_op jit(solution)/shard_map/psum | solution.py:69
  362.6 1.7 reduce-scatter.5.cloned.1.call-done
  364.4 0.0 copy-done.3
  364.4 0.0 copy-done.6
  364.4 0.0 copy-done.7
  364.4 1.0 fusion.39
  365.4 14.1 %all-reduce = (f32[2,128]{1,0:T(2,128)S(1)}, f32[2,128]{1,0:T(2,128)S(1)}) all-reduce(f32[2,128]{1,0:T(2,128)S(1)} %get-tuple-element.8, f32[2,128]{1,0:T(2,128)S(1)} %get-tuple-element.7), channel_id=1, replica_groups=mesh['batch'=8,'col'=32] {'batch'}, use_global_device_ids=true, to_apply=%region_18.19 | all-reduce | flops 512 | bytes 4096 | tf_op jit(solution)/shard_map/psum | solution.py:84
  379.5 0.5 reduce_sum.137
  380.1 0.5 broadcast_multiply_fusion.3
  380.6 0.7 fusion.31
  381.3 42.5 %reduce-scatter.3.cloned.1.call-done = f32[512,256]{1,0:T(8,128)} async-done(((f32[4096,256]{1,0:T(8,128)}), f32[512,256]{1,0:T(8,128)}) %reduce-scatter.3.cloned.1.call-update) | async-done | bytes 524304 | tf_op jit(solution)/shard_map/reduce_scatter | solution.py:77
  (11 shorter events, 0.0 us)
Async XLA Ops:
  7.2 88.0 %copy-start = (bf16[4096,256]{1,0:T(8,128)(2,1)S(1)}, bf16[4096,256]{1,0:T(8,128)(2,1)}, u32[]{:S(2)}) copy-start(bf16[4096,256]{1,0:T(8,128)(2,1)} %param.7) | copy-start | bytes 6291460
  7.2 88.0 %all-gather.3.cloned.1.call-start = ((), (), s32[]{:S(2)}) async-start(), calls=%async_computation.2 | async-start | bytes 2162688 | tf_op jit(solution)/shard_map/all_gather | solution.py:32
  38.8 92.3 %all-gather.5.cloned.1.call-start = ((), (), s32[]{:S(2)}) async-start(), calls=%async_computation.3 | async-start | bytes 1179648 | tf_op jit(solution)/shard_map/all_gather | solution.py:36
  98.2 157.7 %all-reduce.3.cloned.1.call-start = ((), (), s32[]{:S(2)}) async-start(), calls=%async_computation.4 | async-start | bytes 2097152 | tf_op jit(solution)/shard_map/psum | solution.py:48
  131.1 5.0 %copy-start.1 = (bf16[2,1024,256]{2,1,0:T(8,128)(2,1)S(1)}, bf16[2,1024,256]{2,1,0:T(8,128)(2,1)}, u32[]{:S(2)}) copy-start(bf16[2,1024,256]{2,1,0:T(8,128)(2,1)} %all-gather.5.cloned.1.call-done) | copy-start | bytes 3145732
  134.6 1.4 copy-start.2
  137.5 226.9 %reduce-scatter.5.cloned.1.call-start = ((), (), s32[]{:S(2)}) async-start(), calls=%async_computation.6 | async-start | bytes 4325376 | tf_op jit(solution)/shard_map/reduce_scatter | solution.py:70
  138.8 133.1 %copy-start.5 = (f32[1,128,256]{2,1,0:T(8,128)S(1)}, f32[1,128,256]{2,1,0:T(8,128)}, u32[]{:S(2)}) copy-start(f32[1,128,256]{2,1,0:T(8,128)} %get-tuple-element.13) | copy-start | bytes 393220
  275.7 148.1 %reduce-scatter.3.cloned.1.call-start = ((), (), s32[]{:S(2)}) async-start(), calls=%async_computation.5 | async-start | bytes 4718592 | tf_op jit(solution)/shard_map/reduce_scatter | solution.py:77
  280.0 2.7 copy-start.4
  280.0 84.3 %copy-start.3 = (bf16[2,128,128]{2,1,0:T(8,128)(2,1)S(1)}, bf16[2,128,128]{2,1,0:T(8,128)(2,1)}, u32[]{:S(2)}) copy-start(bf16[2,128,128]{2,1,0:T(8,128)(2,1)} %param.4) | copy-start | bytes 196612
  280.0 84.3 %copy-start.6 = (f32[128]{0:T(128)S(1)}, f32[128]{0:T(128)}, u32[]{:S(2)}) copy-start(f32[128]{0:T(128)} %param.5) | copy-start | bytes 1540
  280.0 84.3 %copy-start.7 = (f32[128]{0:T(128)S(1)}, f32[128]{0:T(128)}, u32[]{:S(2)}) copy-start(f32[128]{0:T(128)} %param.6) | copy-start | bytes 1540
Sparse Core Ops, SparseCore 0:
  38.9 56.2 all-gather.2
  98.3 32.7 all-gather.4
  137.6 118.2 all-reduce.2
  275.8 88.5 reduce-scatter.4
  367.3 56.3 reduce-scatter.2
where the time goes:
time: 431 us; the launch traced here: 430 us
  waiting for transfers between devices  249 us (58%)
  blocking collectives  134 us (31%)
  between operations  16.5 us (4%)
  other arithmetic  14.9 us (3%)
  matrix products  13.8 us (3%)
    psum x1, waiting for transfers between devices, shards(): kernel = lax.psum(kernel_part, 'col')  116 us
    psum x1, blocking collectives, shards(): loss = lax.psum(share, ('batch', 'col'))  78.4 us
    all_gather x1, waiting for transfers between devices, shards(): act_full = lax.all_gather(act, 'col', axis=2, tiled=True)  56.4 us
    reduce_scatter x1, waiting for transfers between devices, shards(): lax.psum_scatter(jnp.einsum('vrk,vrj->kj', act_full, dzb, preferred_eleme...  42.5 us
    all_gather x1, waiting for transfers between devices, shards(): z_all = lax.all_gather(z_local, 'batch', axis=1, tiled=True)  32.8 us
    psum x1, blocking collectives, shards(): total = lax.psum(jnp.sum(hidden_float, axis=1), 'batch')  17.3 us
    psum x1, blocking collectives, shards(): lax.psum((jnp.sum(preactivation_gradient, axis=1), jnp.sum(preactivation_...  14.1 us
    psum x1, blocking collectives, shards(): col_total = lax.psum(jnp.sum(summed, axis=1), 'batch')  13.7 us
  transfers between devices with their start and end apart: 5, of which 5 were waited for; matrix products, arithmetic and copies ran while one was open for 3% of the time, Pallas kernels for 0%

commit v1 on v0

--- a/solution.py
+++ b/solution.py
@@ -33,7 +33,9 @@
     z_local = jnp.einsum(
         "vrk,kj->vrj", act_full, weight, preferred_element_type=jnp.float32
     ).astype(jnp.bfloat16)
-    z_all = lax.all_gather(z_local, "batch", axis=1, tiled=True)
+    z_all = jnp.concatenate(
+        lax.all_to_all(jnp.stack([z_local] * lax.axis_size("batch")), "batch", 0, 0), axis=1
+    )
     zf_all = z_all.astype(jnp.float32)
     zmean = jnp.mean(zf_all, axis=1, keepdims=True)
     zc_all = zf_all - zmean

time: 431 us -> 421 us (0.977)
  waiting for transfers between devices: 249 us -> 238 us
  starting transfers between devices: 0.21 us -> 6.89 us
  other arithmetic: 14.9 us -> 10.5 us
    all_gather x1 -> x0, waiting for transfers between devices: 32.8 us -> none  [shards(): z_all = lax.all_gather(z_local, 'batch', axis=1, tiled=True)]
    all_to_all x0 -> x1, waiting for transfers between devices: none -> 29.2 us  [shards(): lax.all_to_all(jnp.stack([z_local] * lax.axis_size('batch')), 'batch', 0, 0)]
    psum x1, waiting for transfers between devices: 116 us -> 107 us  [shards(): kernel = lax.psum(kernel_part, 'col')]
    all_to_all x0 -> x1, starting transfers between devices: none -> 6.73 us  [shards(): lax.all_to_all(jnp.stack([z_local] * lax.axis_size('batch')), 'batch', 0, 0)]
where the time goes in v1:
time: 421 us
  waiting for transfers between devices  238 us (57%)
  blocking collectives  134 us (32%)
  between operations  16.6 us (4%)
  matrix products  13 us (3%)
  other arithmetic  10.5 us (2%)
  starting transfers between devices  6.89 us (2%)
    psum x1, waiting for transfers between devices, shards(): kernel = lax.psum(kernel_part, 'col')  107 us
    psum x1, blocking collectives, shards(): loss = lax.psum(share, ('batch', 'col'))  78.4 us
    all_gather x1, waiting for transfers between devices, shards(): act_full = lax.all_gather(act, 'col', axis=2, tiled=True)  56.4 us
    reduce_scatter x1, waiting for transfers between devices, shards(): lax.psum_scatter(jnp.einsum('vrk,vrj->kj', act_full, dzb, preferred_eleme...  42.9 us
    all_to_all x1, waiting for transfers between devices, shards(): lax.all_to_all(jnp.stack([z_local] * lax.axis_size('batch')), 'batch', 0, 0)  29.2 us
    psum x1, blocking collectives, shards(): total = lax.psum(jnp.sum(hidden_float, axis=1), 'batch')  17.3 us
    psum x1, blocking collectives, shards(): col_total = lax.psum(jnp.sum(summed, axis=1), 'batch')  13.7 us
    psum x1, blocking collectives, shards(): lax.psum((jnp.sum(preactivation_gradient, axis=1), jnp.sum(preactivation_...  13.4 us
  transfers between devices with their start and end apart: 5, of which 5 were waited for; matrix products, arithmetic and copies ran while one was open for 3% of the time, Pallas kernels for 0%

profile of v1, /device:TPU:1, one launch (start us, length us, event | category | flops | bytes accessed | tf_op | source)
XLA Modules:
  0.0 420.7 jit_solution(186589146779951502)
XLA Ops:
  7.2 0.0 copy-start
  7.2 0.0 all-gather.2.cloned.1.call-start
  7.2 1.0 convert_reduce_fusion
  8.2 17.3 %psum.49 = f32[2,128]{1,0:T(2,128)S(1)} all-reduce(f32[2,128]{1,0:T(2,128)S(1)} %convert_reduce_fusion), channel_id=1, replica_groups=mesh['batch'=8,'col'=32] {'batch'}, use_global_device_ids=true, to_apply=%region_1.0 | all-reduce | flops 256 | bytes 2048 | tf_op jit(solution)/shard_map/psum | solution.py:23
  25.5 0.9 fusion.32
  26.4 10.8 %psum.50 = f32[2,128]{1,0:T(2,128)S(1)} all-reduce(f32[2,128]{1,0:T(2,128)S(1)} %fusion.32), channel_id=1, replica_groups=mesh['batch'=8,'col'=32] {'batch'}, use_global_device_ids=true, to_apply=%region_3.0 | all-reduce | flops 256 | bytes 2048 | tf_op jit(solution)/shard_map/psum | solution.py:26
  37.2 1.6 fusion.25
  38.8 0.0 all-gather.2.cloned.1.call-update
  38.8 56.4 %all-gather.2.cloned.1.call-done = bf16[2,128,4096]{2,1,0:T(8,128)(2,1)} async-done(((bf16[2,128,128]{2,1,0:T(8,128)(2,1)}), bf16[2,128,4096]{2,1,0:T(8,128)(2,1)}) %all-gather.2.cloned.1.call-update) | async-done | bytes 2097168 | tf_op jit(solution)/shard_map/all_gather | solution.py:32
  95.2 0.0 copy-done
  95.2 2.3 fusion.42
  97.5 1.1 stack.4
  98.6 6.7 %all-to-all-start = ((bf16[8,2,128,256]{3,2,1,0:T(8,128)(2,1)}), bf16[8,2,128,256]{3,2,1,0:T(8,128)(2,1)S(1)}, u32[]{:S(2)}, u32[]{:S(2)}) async-start(bf16[8,2,128,256]{3,2,1,0:T(8,128)(2,1)} %stack.4), calls=%async_computation | async-start | bytes 2097152 | tf_op jit(solution)/shard_map/all_to_all | solution.py:37
  105.3 0.0 all-reduce.3.cloned.1.call-start
  105.4 29.2 %all-to-all-done = bf16[8,2,128,256]{3,2,1,0:T(8,128)(2,1)S(1)} async-done(((bf16[8,2,128,256]{3,2,1,0:T(8,128)(2,1)}), bf16[8,2,128,256]{3,2,1,0:T(8,128)(2,1)S(1)}, u32[]{:S(2)}, u32[]{:S(2)}) %all-to-all-start) | async-done | bytes 1048608 | tf_op jit(solution)/shard_map/all_to_all | solution.py:37
  134.6 0.2 fusion.3
  134.8 0.2 convert_bitcast_fusion
  135.0 0.2 copy.10
  135.2 0.1 bitcast_subtract_fusion
  135.3 0.0 copy-start.1
  135.3 1.3 copy-done.1
  136.7 1.5 fusion.11
  138.1 0.0 all-reduce.3.cloned.1.call-update
  138.2 0.0 reduce-scatter.5.cloned.1.call-start
  138.2 1.3 fusion.41
  139.5 0.3 multiply_reduce_fusion
  139.8 0.6 fusion.37
  140.4 107.0 %all-reduce.3.cloned.1.call-done = f32[2,128,1024]{2,1,0:T(8,128)} async-done(((f32[2,128,1024]{2,1,0:T(8,128)}), f32[2,128,1024]{2,1,0:T(8,128)}) %all-reduce.3.cloned.1.call-update) | async-done | bytes 1048592 | tf_op jit(solution)/shard_map/psum | solution.py:50
  247.4 2.2 fusion.43
  249.6 13.7 %psum.53 = f32[2,256]{1,0:T(2,128)S(1)} all-reduce(f32[2,256]{1,0:T(2,128)S(1)} %get-tuple-element.22), channel_id=1, replica_groups=mesh['batch'=8,'col'=32] {'batch'}, use_global_device_ids=true, to_apply=%region_14.15 | all-reduce | flops 512 | bytes 4096 | tf_op jit(solution)/shard_map/psum | solution.py:60
  263.3 0.0 copy-done.4
  263.4 2.7 convolution_bitcast_fusion
  266.1 0.0 reduce-scatter.5.cloned.1.call-update
  266.1 0.0 reduce-scatter.3.cloned.1.call-start
  266.2 4.3 %convolution_bitcast_fusion.1 = f32[4096,256]{1,0:T(8,128)} fusion(bf16[2,128,4096]{2,1,0:T(8,128)(2,1)} %all-gather.2.cloned.1.call-done, bf16[2,128,256]{2,1,0:T(8,128)(2,1)S(1)} %fusion.13), kind=kOutput, calls=%fused_computation.1 | convolution fusion | flops 536870912 | bytes 6422528 | tf_op jit(solution)/shard_map/vrk,vrj->kj/dot_general | solution.py:80
  270.5 0.0 reduce-scatter.3.cloned.1.call-update
  271.9 0.6 multiply_reduce_fusion.4
  273.1 0.0 copy-done.2
  273.1 0.9 multiply_reduce_fusion.2
  274.7 78.4 %psum.52 = f32[]{:T(128)} all-reduce(f32[]{:T(128)S(6)} %add.83), channel_id=1, replica_groups=mesh['batch'=8,'col'=32] {'batch','col'}, use_global_device_ids=true, to_apply=%region_12.13 | all-reduce | flops 1 | bytes 8 | tf_op jit(solution)/shard_map/psum | solution.py:71
  353.1 2.0 reduce-scatter.5.cloned.1.call-done
  355.1 0.0 copy-done.5
  355.1 1.0 fusion.39
  356.1 13.4 %all-reduce = (f32[2,128]{1,0:T(2,128)S(1)}, f32[2,128]{1,0:T(2,128)S(1)}) all-reduce(f32[2,128]{1,0:T(2,128)S(1)} %get-tuple-element.8, f32[2,128]{1,0:T(2,128)S(1)} %get-tuple-element.7), channel_id=1, replica_groups=mesh['batch'=8,'col'=32] {'batch'}, use_global_device_ids=true, to_apply=%region_18.19 | all-reduce | flops 512 | bytes 4096 | tf_op jit(solution)/shard_map/psum | solution.py:86
  369.5 0.5 reduce_sum.137
  370.1 0.5 broadcast_multiply_fusion.3
  370.6 0.7 fusion.31
  371.3 42.9 %reduce-scatter.3.cloned.1.call-done = f32[512,256]{1,0:T(8,128)} async-done(((f32[4096,256]{1,0:T(8,128)}), f32[512,256]{1,0:T(8,128)}) %reduce-scatter.3.cloned.1.call-update) | async-done | bytes 524304 | tf_op jit(solution)/shard_map/reduce_scatter | solution.py:79
  (12 shorter events, 0.1 us)
Async XLA Ops:
  7.2 88.0 %copy-start = (bf16[4096,256]{1,0:T(8,128)(2,1)S(1)}, bf16[4096,256]{1,0:T(8,128)(2,1)}, u32[]{:S(2)}) copy-start(bf16[4096,256]{1,0:T(8,128)(2,1)} %param.7) | copy-start | bytes 6291460
  7.2 88.0 %all-gather.2.cloned.1.call-start = ((), (), s32[]{:S(2)}) async-start(), calls=%async_computation.3 | async-start | bytes 2162688 | tf_op jit(solution)/shard_map/all_gather | solution.py:32
  98.6 36.0 %all-to-all-start = ((bf16[8,2,128,256]{3,2,1,0:T(8,128)(2,1)}), bf16[8,2,128,256]{3,2,1,0:T(8,128)(2,1)S(1)}, u32[]{:S(2)}, u32[]{:S(2)}) async-start(bf16[8,2,128,256]{3,2,1,0:T(8,128)(2,1)} %stack.4), calls=%async_computation | async-start | bytes 2097152 | tf_op jit(solution)/shard_map/all_to_all | solution.py:37
  105.3 142.0 %all-reduce.3.cloned.1.call-start = ((), (), s32[]{:S(2)}) async-start(), calls=%async_computation.4 | async-start | bytes 2097152 | tf_op jit(solution)/shard_map/psum | solution.py:50
  135.3 1.4 copy-start.1
  138.2 216.9 %reduce-scatter.5.cloned.1.call-start = ((), (), s32[]{:S(2)}) async-start(), calls=%async_computation.6 | async-start | bytes 4325376 | tf_op jit(solution)/shard_map/reduce_scatter | solution.py:72
  139.5 123.8 %copy-start.4 = (f32[1,128,256]{2,1,0:T(8,128)S(1)}, f32[1,128,256]{2,1,0:T(8,128)}, u32[]{:S(2)}) copy-start(f32[1,128,256]{2,1,0:T(8,128)} %get-tuple-element.13) | copy-start | bytes 393220
  266.1 148.1 %reduce-scatter.3.cloned.1.call-start = ((), (), s32[]{:S(2)}) async-start(), calls=%async_computation.5 | async-start | bytes 4718592 | tf_op jit(solution)/shard_map/reduce_scatter | solution.py:79
  270.4 2.7 copy-start.2
  270.5 84.6 %copy-start.3 = (bf16[2,128,128]{2,1,0:T(8,128)(2,1)S(1)}, bf16[2,128,128]{2,1,0:T(8,128)(2,1)}, u32[]{:S(2)}) copy-start(bf16[2,128,128]{2,1,0:T(8,128)(2,1)} %param.4) | copy-start | bytes 196612
  270.5 84.6 %copy-start.5 = (f32[128]{0:T(128)S(1)}, f32[128]{0:T(128)}, u32[]{:S(2)}) copy-start(f32[128]{0:T(128)} %param.5) | copy-start | bytes 1540
  270.5 84.6 %copy-start.6 = (f32[128]{0:T(128)S(1)}, f32[128]{0:T(128)}, u32[]{:S(2)}) copy-start(f32[128]{0:T(128)} %param.6) | copy-start | bytes 1540
Sparse Core Ops, SparseCore 0:
  38.9 56.2 all-gather.1
  138.3 109.0 all-reduce.2
  266.2 88.7 reduce-scatter.4
  358.0 56.1 reduce-scatter.2
